TPU v7x, 32 devices: a whole 2x2x4 slice. The times are simulated.
32 devices in a mesh: dp: 4 (over y, x), mp: 8 (over z, core).
Axes of the slice: x: 2, y: 2, z: 4, core: 2. Of those that a mesh axis runs over, the one named last changes fastest.
Arguments:
- tokens: bfloat16 [1024, 4096], P('dp', 'mp'), may hold values from -6 to 6
- cotangent: bfloat16 [1024, 4096], P('dp', 'mp'), may hold values from -6 to 6
- gate_weight: bfloat16 [4096, 16384], P('dp', 'mp'), may hold values from -0.1875 to 0.1875
- up_weight: bfloat16 [4096, 16384], P('dp', 'mp'), may hold values from -0.1875 to 0.1875
- down_weight: bfloat16 [16384, 4096], P('mp', 'dp'), may hold values from -0.09375 to 0.09375
- gate_mask: int32 [32, 128], P('dp', 'mp'), may hold values from 0 to 1, as said below
- up_mask: int32 [32, 128], P('dp', 'mp'), may hold values from 0 to 1, as said below
- down_mask: int32 [128, 32], P('mp', 'dp'), may hold values from 0 to 1, as said below
Outputs:
- layer_out: bfloat16 [1024, 4096], P('dp', 'mp')
- token_grad: bfloat16 [1024, 4096], P('dp', 'mp')
- gate_grad: bfloat16 [4096, 16384], P('dp', 'mp')
- up_grad: bfloat16 [4096, 16384], P('dp', 'mp')
- down_grad: bfloat16 [16384, 4096], P('mp', 'dp')
Inputs may be any that keep to these rules, and one draw needn't show every extreme that they name: `gate_mask`: each device's part of the mask (8 x 16 blocks) has 1 to 64 nonzero blocks; in every draw all parts of one index of mp, chosen by the seed, have exactly 64, the same index for the three masks. `up_mask`: each device's part of the mask (8 x 16 blocks) has 1 to 64 nonzero blocks; in every draw all parts of one index of mp, chosen by the seed, have exactly 64, the same index for the three masks. `down_mask`: each device's part of the mask (16 x 8 blocks) has 1 to 64 nonzero blocks; in every draw all parts of one index of mp, chosen by the seed, have exactly 64, the same index for the three masks.
All inputs are finite; a program needn't handle non-finite values.
Results may differ from a plain program's by a relative error of at most 0.017.
Values may be sent and summed in bfloat16 or wider, within the bound.
No kernel may reach another device: no remote copies, remote signals or barrier semaphores. Data moves between devices by JAX's collectives and lax.ppermute only.
A program may use at most 192 MiB of HBM per device.

v0:
```python
import math

import jax
import jax.numpy as jnp
from jax import lax
from jax.sharding import PartitionSpec as P

BLK = 128


def to_tiles(matrix, tile_size):
    row_count = matrix.shape[0] // tile_size
    col_count = matrix.shape[1] // tile_size
    shaped = matrix.reshape(row_count, tile_size, col_count, tile_size).transpose(0, 2, 1, 3)
    return shaped.reshape(row_count * col_count, tile_size * tile_size)


def from_tiles(tile_rows, row_count, col_count, tile_size):
    shaped = tile_rows.reshape(row_count, col_count, tile_size, tile_size).transpose(0, 2, 1, 3)
    return shaped.reshape(row_count * tile_size, col_count * tile_size)


def body(tokens, cotangent, gate_weight, up_weight, down_weight, gate_mask, up_mask, down_mask):
    tile_size = BLK
    local_rows = tokens.shape[0]
    dp_count = lax.axis_size("dp")
    full_tokens, full_cotangent = (
        lax.all_gather(tokens, "mp", axis=1, tiled=True),
        lax.all_gather(cotangent, "mp", axis=1, tiled=True),
    )
    row_tiles = gate_weight.shape[0] // tile_size
    col_tiles = gate_weight.shape[1] // tile_size
    tile_count = row_tiles * col_tiles
    capacity = tile_count // 2
    shards = [gate_weight, up_weight, down_weight.T]
    mask_table = jnp.stack(
        [
            gate_mask.reshape(tile_count),
            up_mask.reshape(tile_count),
            down_mask.T.reshape(tile_count),
        ]
    )
    slot_of = jnp.cumsum(mask_table, axis=1) - 1
    own_slot = jnp.where(mask_table > 0, slot_of, 0)
    slot_hits = (slot_of[:, None, :] == jnp.arange(capacity, dtype=jnp.int32)[None, :, None]) & (
        mask_table[:, None, :] > 0
    )
    tile_index = jnp.arange(tile_count, dtype=jnp.int32)
    own_ids = jnp.where(
        jnp.any(slot_hits, axis=2),
        jnp.sum(jnp.where(slot_hits, tile_index[None, None, :], 0), axis=2),
        -1,
    )
    packed_list = []
    for matrix in range(3):
        chosen = jnp.take(
            to_tiles(shards[matrix], tile_size), jnp.maximum(own_ids[matrix], 0), axis=0
        )
        packed_list.append(
            jnp.where((own_ids[matrix] >= 0)[:, None], chosen, jnp.zeros_like(chosen))
        )
    packed = jnp.stack(packed_list, axis=0)
    all_tiles, all_ids = (
        lax.all_gather(packed, "dp", axis=1, tiled=True),
        lax.all_gather(own_ids, "dp", axis=1, tiled=True),
    )
    slot_total = dp_count * capacity
    anchor = jnp.arange(slot_total, dtype=jnp.int32) // capacity
    global_ids = jnp.where(all_ids >= 0, anchor[None, :] * tile_count + all_ids, -1)
    grid_count = dp_count * tile_count
    grid_index = jnp.arange(grid_count, dtype=jnp.int32)
    holder = global_ids[:, None, :] == grid_index[None, :, None]
    slot_index = jnp.arange(slot_total, dtype=jnp.int32)
    has_tile = jnp.any(holder, axis=2)
    holder_slot = jnp.sum(jnp.where(holder, slot_index[None, None, :], 0), axis=2)
    dense_list = []
    for matrix in range(3):
        chosen = jnp.take(all_tiles[matrix], holder_slot[matrix], axis=0)
        chosen = jnp.where(has_tile[matrix][:, None], chosen, jnp.zeros_like(chosen))
        dense_list.append(from_tiles(chosen, dp_count * row_tiles, col_tiles, tile_size))
    gate_full, up_full, down_full = dense_list
    gate_pre = jnp.dot(full_tokens, gate_full, preferred_element_type=jnp.float32)
    up_pre = jnp.dot(full_tokens, up_full, preferred_element_type=jnp.float32)
    sigmoid_gate = 1.0 / (1.0 + jnp.exp(-gate_pre))
    activated = gate_pre * sigmoid_gate
    hidden = (activated * up_pre).astype(jnp.bfloat16)
    contract_last = (((1,), (1,)), ((), ()))
    output_term = lax.dot_general(
        hidden, down_full, contract_last, preferred_element_type=jnp.float32
    )
    layer_out = lax.psum_scatter(
        output_term.astype(jnp.bfloat16), "mp", scatter_dimension=1, tiled=True
    )
    hidden_grad = jnp.dot(full_cotangent, down_full, preferred_element_type=jnp.float32)
    gate_delta = (
        hidden_grad * up_pre * sigmoid_gate * (1.0 + gate_pre * (1.0 - sigmoid_gate))
    ).astype(jnp.bfloat16)
    up_delta = (hidden_grad * activated).astype(jnp.bfloat16)
    input_term = lax.dot_general(
        gate_delta, gate_full, contract_last, preferred_element_type=jnp.float32
    ) + lax.dot_general(up_delta, up_full, contract_last, preferred_element_type=jnp.float32)
    token_grad = lax.psum_scatter(
        input_term.astype(jnp.bfloat16), "mp", scatter_dimension=1, tiled=True
    )
    left_terms = [full_tokens, full_tokens, full_cotangent]
    right_terms = [gate_delta, up_delta, hidden]
    live_slot = global_ids >= 0
    clipped = jnp.where(live_slot, global_ids, 0)
    blocks_out = []
    for matrix in range(3):
        left_view = left_terms[matrix].reshape(local_rows, dp_count * row_tiles, tile_size)
        right_view = right_terms[matrix].reshape(local_rows, col_tiles, tile_size)
        dense_tiles = jnp.einsum(
            "ria,rjb->ijab", left_view, right_view, preferred_element_type=jnp.float32
        )
        dense_tiles = dense_tiles.reshape(grid_count, tile_size * tile_size)
        chosen = jnp.take(dense_tiles, clipped[matrix], axis=0)
        blocks_out.append(jnp.where(live_slot[matrix][:, None], chosen, 0.0))
    picked = jnp.stack(blocks_out, axis=0)
    summed = lax.psum_scatter(
        picked.reshape(3, dp_count, capacity, tile_size * tile_size).astype(jnp.bfloat16),
        "dp",
        scatter_dimension=1,
        tiled=True,
    ).astype(jnp.float32)
    grad_scale = 1.0 / math.sqrt(local_rows * dp_count)
    own_grads = (summed[:, 0] * grad_scale).astype(jnp.bfloat16)
    grad_shards = []
    for matrix in range(3):
        chosen = jnp.take(own_grads[matrix], own_slot[matrix], axis=0)
        chosen = jnp.where((mask_table[matrix] > 0)[:, None], chosen, jnp.zeros_like(chosen))
        grad_shards.append(from_tiles(chosen, row_tiles, col_tiles, tile_size))
    return (layer_out, token_grad, grad_shards[0], grad_shards[1], grad_shards[2].T)


def solution(mesh):
    placed = (
        P("dp", "mp"),
        P("dp", "mp"),
        P("dp", "mp"),
        P("dp", "mp"),
        P("mp", "dp"),
        P("dp", "mp"),
        P("dp", "mp"),
        P("mp", "dp"),
    )
    return jax.shard_map(
        body,
        mesh=mesh,
        in_specs=placed,
        out_specs=(P("dp", "mp"), P("dp", "mp"), P("dp", "mp"), P("dp", "mp"), P("mp", "dp")),
        check_vma=False,
    )
```

profile of v0, /device:TPU:6, one launch (start us, length us, event | category | flops | bytes accessed | tf_op | source)
XLA Modules:
  0.0 1375.0 jit_solution(1911390987535153168)
XLA Ops:
  91.8 211.6 %all-gather.5.cloned.1.call-done = bf16[3,256,16384]{2,1,0:T(8,128)(2,1)} async-done(((bf16[3,64,16384]{2,1,0:T(8,128)(2,1)}), bf16[3,256,16384]{2,1,0:T(8,128)(2,1)}) %all-gather.5.cloned.1.call-update) | async-done | bytes 25165840 | tf_op jit(solution)/shard_map/all_gather | solution.py:64
  303.4 17.7 %slice_bitcast_fusion = (bf16[256,16384]{1,0:T(8,128)(2,1)}, bf16[256,16384]{1,0:T(8,128)(2,1)}, bf16[256,16384]{1,0:T(8,128)(2,1)}) fusion(bf16[3,256,16384]{2,1,0:T(8,128)(2,1)} %all-gather.5.cloned.1.call-done), kind=kLoop, calls=%fused_computation.50 | loop fusion | bytes 50331648 | tf_op jit(solution)/shard_map/squeeze | solution.py:78
  321.0 43.8 %gather_fusion.5 = bf16[512,16384]{1,0:T(8,128)(2,1)} fusion(bf16[256,16384]{1,0:T(8,128)(2,1)} %get-tuple-element.31, s32[1024]{0:T(1024)S(1)} %pad_clamp_fusion.6), kind=kCustom, calls=%fused_computation.7.clone | custom fusion | bytes 33556480 | tf_op jit(solution)/shard_map/jit(_take)/gather | solution.py:78
  364.8 34.0 %gather_fusion.4 = bf16[512,16384]{1,0:T(8,128)(2,1)} fusion(bf16[256,16384]{1,0:T(8,128)(2,1)} %get-tuple-element.32, s32[1024]{0:T(1024)S(1)} %pad_clamp_fusion.7), kind=kCustom, calls=%fused_computation.6.clone | custom fusion | bytes 33556480 | tf_op jit(solution)/shard_map/jit(_take)/gather | solution.py:78
  398.8 9.4 fusion.15
  425.5 19.1 %copy.63 = bf16[32,16,128,128]{3,1,2,0:T(8,128)(2,1)} copy(bf16[32,16,128,128]{3,2,1,0:T(8,128)(2,1)} %bitcast.261) | data formatting | bytes 33554432 | tf_op jit(solution)/shard_map/reshape | solution.py:19
  447.9 12.1 copy.62
  460.0 33.8 %gather_fusion.3 = bf16[512,16384]{1,0:T(8,128)(2,1)} fusion(bf16[256,16384]{1,0:T(8,128)(2,1)} %get-tuple-element.33, s32[1024]{0:T(1024)S(1)} %copy-done.14), kind=kCustom, calls=%fused_computation.1.clone | custom fusion | bytes 33556480 | tf_op jit(solution)/shard_map/jit(_take)/gather | solution.py:78
  505.9 12.1 copy.60
  518.1 15.8 %fusion.42 = f32[256,2048]{0,1:T(8,128)} fusion(bf16[256,4096]{0,1:T(8,128)(2,1)} %all-gather.9.cloned.1.call-done, bf16[512,8,16,128]{3,2,1,0:T(8,128)(2,1)} %bitcast.274), kind=kOutput, calls=%fused_computation.74 | convolution fusion | flops 4294967296 | bytes 20971520 | tf_op jit(solution)/shard_map/dot_general | solution.py:94
  533.9 16.2 %fusion.39 = f32[256,2048]{0,1:T(8,128)} fusion(bf16[256,4096]{0,1:T(8,128)(2,1)} %all-gather.7.cloned.1.call-done, bf16[512,8,16,128]{3,2,1,0:T(8,128)(2,1)} %bitcast.270), kind=kOutput, calls=%fused_computation.73 | convolution fusion | flops 4294967296 | bytes 20971520 | tf_op jit(solution)/shard_map/dot_general | solution.py:83
  550.1 15.1 %multiply_convert_fusion.2 = (bf16[256,2048]{0,1:T(8,128)(2,1)S(1)}, bf16[256,2048]{0,1:T(8,128)(2,1)}, bf16[256,2048]{0,1:T(8,128)(2,1)}) fusion(f32[256,2048]{0,1:T(8,128)} %fusion.42, f32[256,2048]{0,1:T(8,128)} %fusion.39, bf16[256,4096]{0,1:T(8,128)(2,1)} %all-gather.7.cloned.1.call-done, bf16[512,8,16,128]{3,2,1,0:T(8,128)(2,1)S(1)} %bitcast.273), kind=kOutput, calls=%fused_computation.85 | convolution fusion | flops 4302831616 | bytes 26214400 | tf_op jit(solution)/shard_map/dot_general | solution.py:82
  565.2 9.8 convolution_bitcast_fusion
  575.1 22.5 %copy.70 = bf16[32,16,128,128]{3,2,1,0:T(8,128)(2,1)} copy(bf16[32,16,128,128]{2,3,0,1:T(8,128)(2,1)} %convolution_bitcast_fusion) | data formatting | bytes 33554432 | tf_op jit(solution)/shard_map/ria,rjb->ijab/transpose | solution.py:113
  597.6 19.4 %copy.153 = bf16[64,8,128,128]{3,1,2,0:T(8,128)(2,1)} copy(bf16[64,8,128,128]{3,2,1,0:T(8,128)(2,1)} %bitcast.264) | data formatting | bytes 33554432
  625.2 22.5 %copy.68 = bf16[32,16,128,128]{3,2,1,0:T(8,128)(2,1)} copy(bf16[32,16,128,128]{2,3,0,1:T(8,128)(2,1)} %convolution_bitcast_fusion.1) | data formatting | bytes 33554432 | tf_op jit(solution)/shard_map/ria,rjb->ijab/transpose | solution.py:113
  647.7 19.3 %copy.154 = bf16[64,8,128,128]{3,1,2,0:T(8,128)(2,1)} copy(bf16[64,8,128,128]{3,2,1,0:T(8,128)(2,1)} %bitcast.265) | data formatting | bytes 33554432
  675.0 22.5 %copy.66 = bf16[32,16,128,128]{3,2,1,0:T(8,128)(2,1)} copy(bf16[32,16,128,128]{2,3,0,1:T(8,128)(2,1)} %convolution_bitcast_fusion.2) | data formatting | bytes 33554432 | tf_op jit(solution)/shard_map/ria,rjb->ijab/transpose | solution.py:113
  697.6 19.7 %copy.155 = bf16[64,8,128,128]{3,1,2,0:T(8,128)(2,1)} copy(bf16[64,8,128,128]{3,2,1,0:T(8,128)(2,1)} %bitcast.266) | data formatting | bytes 33554432
  717.3 24.6 %gather_fusion.8 = bf16[256,16384]{1,0:T(8,128)(2,1)} fusion(bf16[512,16384]{1,0:T(8,128)(2,1)} %bitcast.253, s32[1024]{0:T(1024)} %pad_clamp_fusion.3), kind=kCustom, calls=%fused_computation.9.clone | custom fusion | bytes 16778240 | tf_op jit(solution)/shard_map/jit(_take)/gather | solution.py:117
  741.9 24.7 %gather_fusion.7 = bf16[256,16384]{1,0:T(8,128)(2,1)} fusion(bf16[512,16384]{1,0:T(8,128)(2,1)} %bitcast.254, s32[1024]{0:T(1024)} %pad_clamp_fusion.4), kind=kCustom, calls=%fused_computation.8.clone | custom fusion | bytes 16778240 | tf_op jit(solution)/shard_map/jit(_take)/gather | solution.py:117
  766.6 24.8 %gather_fusion.6 = bf16[256,16384]{1,0:T(8,128)(2,1)} fusion(bf16[512,16384]{1,0:T(8,128)(2,1)} %bitcast.255, s32[1024]{0:T(1024)} %pad_clamp_fusion.5), kind=kCustom, calls=%fused_computation.2.clone | custom fusion | bytes 16778240 | tf_op jit(solution)/shard_map/jit(_take)/gather | solution.py:117
  791.5 11.3 fusion.12
  802.8 11.3 fusion.13
  814.1 11.6 fusion.14
  825.7 21.0 %pad_maximum_fusion = bf16[3,4,64,16384]{3,2,1,0:T(8,128)(2,1)} fusion(bf16[1,4,64,16384]{3,2,1,0:T(8,128)(2,1)} %bitcast.267, bf16[1,4,64,16384]{3,2,1,0:T(8,128)(2,1)} %bitcast.268, bf16[1,4,64,16384]{3,2,1,0:T(8,128)(2,1)} %bitcast.269), kind=kLoop, calls=%fused_computation.15 | loop fusion | flops 25165824 | bytes 50331648 | tf_op jit(solution)/shard_map/stack | solution.py:119
  847.8 11.9 fusion.30
  860.8 13.0 fusion.4
  873.7 14.0 %fusion.27 = bf16[256,4096]{1,0:T(8,128)(2,1)} fusion(f32[256,4096]{1,0:T(8,128)} %fusion.4, bf16[256,2048]{0,1:T(8,128)(2,1)S(1)} %get-tuple-element.37, bf16[512,8,16,128]{3,2,1,0:T(8,128)(2,1)} %bitcast.272), kind=kOutput, calls=%fused_computation.55 | convolution fusion | flops 4297064448 | bytes 24117248 | tf_op jit(solution)/shard_map/dot_general | solution.py:99
  887.8 402.8 %all-reduce.3.cloned.1.call-done = bf16[3,4,64,16384]{3,2,1,0:T(8,128)(2,1)} async-done(((bf16[3,4,64,16384]{3,2,1,0:T(8,128)(2,1)}), bf16[3,4,64,16384]{3,2,1,0:T(8,128)(2,1)}) %all-reduce.3.cloned.1.call-update) | async-done | bytes 25165840
  1297.6 10.9 gather_fusion.9
  1320.2 10.7 gather_fusion.10
  (171 shorter events, 190.9 us)
Async XLA Ops:
  7.2 296.2 %all-gather.5.cloned.1.call-start = ((), (), s32[]{:S(2)}) async-start(), calls=%async_computation.2 | async-start | bytes 31457280 | tf_op jit(solution)/shard_map/all_gather | solution.py:64
  22.8 7.9 copy-start.4
  33.3 5.7 copy-start.5
  69.4 2.2 copy-start.3
  75.4 442.7 %all-gather.9.cloned.1.call-start = ((), (), s32[]{:S(2)}) async-start(), calls=%async_computation.5 | async-start | bytes 2359296 | tf_op jit(solution)/shard_map/all_gather | solution.py:29
  77.2 456.7 %all-gather.7.cloned.1.call-start = ((), (), s32[]{:S(2)}) async-start(), calls=%async_computation.3 | async-start | bytes 2359296 | tf_op jit(solution)/shard_map/all_gather | solution.py:28
  78.1 1212.4 %all-reduce.3.cloned.1.call-start = ((), (), s32[]{:S(2)}) async-start(), calls=%async_computation.7 | async-start | bytes 50331648
  398.8 10.8 copy-start
  416.9 27.7 %slice-start = ((s8[16777216]{0:T(1024)(128)(4,1)}), s8[4194304]{0:T(1024)(128)(4,1)S(1)}, s32[]{:S(2)}) async-start(s8[16777216]{0:T(1024)(128)(4,1)} %bitcast.259), calls=%async_computation.8 | async-start | bytes 8388608
  416.9 27.7 %slice-start.1 = ((s8[16777216]{0:T(1024)(128)(4,1)}), s8[4194304]{0:T(1024)(128)(4,1)S(1)}, s32[]{:S(2)}) async-start(s8[16777216]{0:T(1024)(128)(4,1)} %bitcast.259), calls=%async_computation.9 | async-start | bytes 8388608
  425.5 19.1 %slice-start.2 = ((s8[16777216]{0:T(1024)(128)(4,1)}), s8[4194304]{0:T(1024)(128)(4,1)S(1)}, s32[]{:S(2)}) async-start(s8[16777216]{0:T(1024)(128)(4,1)} %bitcast.259), calls=%async_computation.10 | async-start | bytes 8388608
  425.5 19.1 %slice-start.3 = ((s8[16777216]{0:T(1024)(128)(4,1)}), s8[4194304]{0:T(1024)(128)(4,1)S(1)}, s32[]{:S(2)}) async-start(s8[16777216]{0:T(1024)(128)(4,1)} %bitcast.259), calls=%async_computation.11 | async-start | bytes 8388608
  447.9 12.2 copy-start.14
  460.0 33.8 %copy-start.19 = (pred[512]{0:T(512)(128)(4,1)S(1)}, pred[512]{0:T(512)(128)(4,1)}, u32[]{:S(2)}) copy-start(pred[512]{0:T(512)(128)(4,1)} %compare_and_fusion.8) | copy-start | bytes 1540
  460.0 33.8 %copy-start.20 = (pred[512]{0:T(512)(128)(4,1)S(1)}, pred[512]{0:T(512)(128)(4,1)}, u32[]{:S(2)}) copy-start(pred[512]{0:T(512)(128)(4,1)} %get-tuple-element.11) | copy-start | bytes 1540
  533.9 16.3 %copy-start.1 = (bf16[32,16,128,128]{3,1,2,0:T(8,128)(2,1)S(1)}, bf16[32,16,128,128]{3,1,2,0:T(8,128)(2,1)}, u32[]{:S(2)}) copy-start(bf16[32,16,128,128]{3,1,2,0:T(8,128)(2,1)} %copy.60) | copy-start | bytes 50331652
  597.6 19.5 %copy-start.2 = (bf16[256,4096]{0,1:T(8,128)(2,1)S(1)}, bf16[256,4096]{0,1:T(8,128)(2,1)}, u32[]{:S(2)}) copy-start(bf16[256,4096]{0,1:T(8,128)(2,1)} %all-gather.7.cloned.1.call-done) | copy-start | bytes 6291460
  597.6 19.5 %copy-start.6 = (bf16[256,2048]{0,1:T(8,128)(2,1)S(1)}, bf16[256,2048]{0,1:T(8,128)(2,1)}, u32[]{:S(2)}) copy-start(bf16[256,2048]{0,1:T(8,128)(2,1)} %get-tuple-element.38) | copy-start | bytes 3145732
  766.6 24.8 %copy-start.18 = (pred[256]{0:T(512)(128)(4,1)S(1)}, pred[256]{0:T(512)(128)(4,1)}, u32[]{:S(2)}) copy-start(pred[256]{0:T(512)(128)(4,1)} %get-tuple-element.14) | copy-start | bytes 772
  766.6 24.8 %copy-start.23 = (pred[256]{0:T(512)(128)(4,1)S(1)}, pred[256]{0:T(512)(128)(4,1)}, u32[]{:S(2)}) copy-start(pred[256]{0:T(512)(128)(4,1)} %compare_and_fusion.3) | copy-start | bytes 772
  791.4 11.3 copy-start.17
  791.4 11.3 copy-start.22
  802.8 11.3 copy-start.16
  802.8 11.3 copy-start.21
  846.6 13.2 copy-start.11
  846.6 13.3 copy-start.12
  846.7 13.4 copy-start.13
  846.7 13.5 copy-start.24
  846.7 14.0 %copy-start.15 = (s32[3,128]{1,0:T(4,128)S(1)}, s32[3,128]{1,0:T(4,128)}, u32[]{:S(2)}) copy-start(s32[3,128]{1,0:T(4,128)} %get-tuple-element.21) | copy-start | bytes 4612
  846.7 14.1 %copy-start.7 = (bf16[256,2048]{0,1:T(8,128)(2,1)S(1)}, bf16[256,2048]{0,1:T(8,128)(2,1)}, u32[]{:S(2)}) copy-start(bf16[256,2048]{0,1:T(8,128)(2,1)} %get-tuple-element.38) | copy-start | bytes 3145732
  846.7 519.5 %reduce-scatter.6.cloned.1.call-start = ((), (), s32[]{:S(2)}) async-start(), calls=%async_computation.4 | async-start | bytes 2359296 | tf_op jit(solution)/shard_map/reduce_scatter | solution.py:91
  859.7 508.0 %reduce-scatter.8.cloned.1.call-start = ((), (), s32[]{:S(2)}) async-start(), calls=%async_computation.6 | async-start | bytes 2359296 | tf_op jit(solution)/shard_map/reduce_scatter | solution.py:102
  (3 other events, 4.0 us)
Sparse Core Ops, SparseCore 0:
  75.5 227.8 all-gather.4
  305.6 30.0 all-gather.8
  337.9 28.5 all-gather.6
  846.8 443.7 all-reduce.2
  1293.2 36.9 reduce-scatter.5
  1333.0 34.7 reduce-scatter.7
where the time goes:
time: 1390 us; the launch traced here: 1380 us
  waiting for transfers between devices  616 us (44%)
  local copies, waits for them, and re-layouts  519 us (37%)
  matrix products  112 us (8%)
  other arithmetic  106 us (8%)
  between operations  15.1 us (1%)
    unnamed x7, waiting for transfers between devices  403 us
    all_gather x1, waiting for transfers between devices, body(): lax.all_gather(packed, 'dp', axis=1, tiled=True)  212 us
    unnamed x80, local copies, waits for them, and re-layouts  125 us
    gather x3, local copies, waits for them, and re-layouts, body(): chosen = jnp.take(all_tiles[matrix], holder_slot[matrix], axis=0)  112 us
    gather x3, local copies, waits for them, and re-layouts, body(): chosen = jnp.take(dense_tiles, clipped[matrix], axis=0)  74.1 us
    transpose x3, local copies, waits for them, and re-layouts, body(): jnp.einsum('ria,rjb->ijab', left_view, right_view, preferred_element_type...  67.5 us
    reshape x3, local copies, waits for them, and re-layouts, from_tiles(): tile_rows.reshape(row_count, col_count, tile_size, tile_size)  43.4 us
    another operation x3, other arithmetic  34.2 us
  transfers between devices with their start and end apart: 6, of which 3 were waited for; matrix products, arithmetic and copies ran while one was open for 26% of the time, Pallas kernels for 0%

commit v1 on v0

v1 whole, which is shorter than its diff:
```python
import math

import jax
import jax.numpy as jnp
from jax import lax
from jax.sharding import PartitionSpec as P

BLK = 128
DP_MODE = "permute"


def spread(mask, width):
    rows, cols = mask.shape
    lane_block = lax.broadcasted_iota(jnp.int32, (cols, width), 1) // (width // cols)
    pick = (lane_block == lax.broadcasted_iota(jnp.int32, (cols, width), 0)).astype(jnp.bfloat16)
    wide = jnp.dot(mask.astype(jnp.bfloat16), pick, preferred_element_type=jnp.float32)
    wide = wide.astype(jnp.bfloat16)
    return jnp.broadcast_to(wide[:, None, :], (rows, BLK, width)).reshape(rows * BLK, width)


def partner(value, bit, dp):
    return lax.ppermute(value, "dp", [(i, i ^ (1 << bit)) for i in range(dp)])


def reduce_over_dp(part, dp, colors=2):
    bits = dp.bit_length() - 1
    cols = part.shape[2] // colors
    done = []
    for color in range(colors):
        order = list(range(bits))
        if color % 2:
            order = order[::-1]
        piece = part[:, :, color * cols : (color + 1) * cols]
        held = list(range(dp))
        vals = {k: piece[k] for k in held}
        for bit in order:
            send = [k for k in held if k >> bit & 1]
            keep = [k for k in held if not k >> bit & 1]
            got = partner(jnp.stack([vals[k].astype(jnp.bfloat16) for k in send]), bit, dp)
            vals = {
                k ^ (1 << bit): vals[k ^ (1 << bit)].astype(jnp.float32) + got[n].astype(jnp.float32)
                for n, k in enumerate(send)
            }
            held = keep
        done.append(vals[0])
    return jnp.concatenate(done, axis=1)


def gather_over_dp(own, dp, colors=2):
    bits = dp.bit_length() - 1
    cols = own.shape[1] // colors
    done = []
    for color in range(colors):
        order = list(range(bits))[::-1]
        if color % 2:
            order = order[::-1]
        vals = {0: own[:, color * cols : (color + 1) * cols]}
        for bit in order:
            held = sorted(vals)
            got = partner(jnp.stack([vals[k] for k in held]), bit, dp)
            for n, k in enumerate(held):
                vals[k ^ (1 << bit)] = got[n]
        done.append(jnp.concatenate([vals[k] for k in range(dp)], axis=0))
    return jnp.concatenate(done, axis=1)


def body(tokens, cotangent, gate_weight, up_weight, down_weight, gate_mask, up_mask, down_mask):
    dp = lax.axis_size("dp")
    mp = lax.axis_size("mp")
    ratio = mp // dp
    rows, cols = tokens.shape
    fan = gate_weight.shape[1]
    bf16, f32 = jnp.bfloat16, jnp.float32
    there = []
    for i in range(dp):
        for j in range(mp):
            d, c = j // ratio, j % ratio
            there.append((i * mp + j, d * mp + ratio * (i ^ d) + c))
    back = [(b, a) for a, b in there]

    def spread_rows(block):
        moved = lax.ppermute(block, ("dp", "mp"), there)
        full = lax.all_gather(moved, "mp", axis=0, tiled=False)
        full = full.reshape(dp, ratio, rows, cols).transpose(0, 2, 1, 3)
        return full.reshape(dp * rows, ratio * cols)

    def collect_rows(part):
        part = part.astype(bf16).reshape(dp, rows, ratio, cols).transpose(0, 2, 1, 3)
        own = lax.psum_scatter(
            part.reshape(mp * rows, cols), "mp", scatter_dimension=0, tiled=True
        )
        return lax.ppermute(own, ("dp", "mp"), back)

    def reduce_dp(part):
        part = part.astype(bf16)
        if DP_MODE == "permute":
            return reduce_over_dp(part.reshape(dp, rows, fan), dp)
        me = lax.axis_index("dp")
        part = part.reshape(dp, rows, fan)[jnp.arange(dp) ^ me]
        return lax.psum_scatter(
            part.reshape(dp * rows, fan), "dp", scatter_dimension=0, tiled=True
        ).astype(f32)

    def gather_dp(own):
        if DP_MODE == "permute":
            return gather_over_dp(own, dp)
        me = lax.axis_index("dp")
        full = lax.all_gather(own, "dp", axis=0, tiled=False)
        return full[jnp.arange(dp) ^ me].reshape(dp * rows, fan)

    gate_keep = spread(gate_mask, fan)
    up_keep = spread(up_mask, fan)
    down_keep = spread(down_mask, down_weight.shape[1])
    gate_eff = gate_weight * gate_keep
    up_eff = up_weight * up_keep
    down_eff = down_weight * down_keep

    tok = spread_rows(tokens)
    cot = spread_rows(cotangent)
    last = (((1,), (1,)), ((), ()))
    first = (((0,), (0,)), ((), ()))

    def dot(a, b, dims=(((1,), (0,)), ((), ()))):
        return lax.dot_general(a, b, dims, preferred_element_type=f32)

    gate_pre = reduce_dp(dot(tok, gate_eff))
    up_pre = reduce_dp(dot(tok, up_eff))
    hidden_grad = reduce_dp(dot(cot, down_eff, last))
    sigmoid_gate = 1.0 / (1.0 + jnp.exp(-gate_pre))
    activated = gate_pre * sigmoid_gate
    hidden = gather_dp((activated * up_pre).astype(bf16))
    gate_delta = gather_dp(
        (hidden_grad * up_pre * sigmoid_gate * (1.0 + gate_pre * (1.0 - sigmoid_gate))).astype(bf16)
    )
    up_delta = gather_dp((hidden_grad * activated).astype(bf16))
    layer_out = collect_rows(dot(hidden, down_eff))
    token_grad = collect_rows(dot(gate_delta, gate_eff, last) + dot(up_delta, up_eff, last))
    scale = 1.0 / math.sqrt(rows * dp)
    gate_grad = (dot(tok, gate_delta, first) * scale * gate_keep.astype(f32)).astype(bf16)
    up_grad = (dot(tok, up_delta, first) * scale * up_keep.astype(f32)).astype(bf16)
    down_grad = (dot(hidden, cot, first) * scale * down_keep.astype(f32)).astype(bf16)
    return (layer_out, token_grad, gate_grad, up_grad, down_grad)


def solution(mesh):
    placed = (
        P("dp", "mp"),
        P("dp", "mp"),
        P("dp", "mp"),
        P("dp", "mp"),
        P("mp", "dp"),
        P("dp", "mp"),
        P("dp", "mp"),
        P("mp", "dp"),
    )
    return jax.shard_map(
        body,
        mesh=mesh,
        in_specs=placed,
        out_specs=(P("dp", "mp"), P("dp", "mp"), P("dp", "mp"), P("dp", "mp"), P("mp", "dp")),
        check_vma=False,
    )
```

time: 1390 us -> 499 us (0.36)
  local copies, waits for them, and re-layouts: 519 us -> 75.6 us
  waiting for transfers between devices: 616 us -> 227 us
  other arithmetic: 106 us -> 12.5 us
  starting transfers between devices: 0.25 us -> 44.1 us
    unnamed x7 -> x4, waiting for transfers between devices: 403 us -> 0.07 us
    gather x12 -> x0, local copies, waits for them, and re-layouts: 234 us -> none  [the longest x3 112 us: body(): chosen = jnp.take(all_tiles[matrix], holder_slot[matrix], axis=0)]
    all_gather x3 -> x2, waiting for transfers between devices: 212 us -> 32.6 us  [spread_rows(): full = lax.all_gather(moved, 'mp', axis=0, tiled=False)]
    ppermute x0 -> x28, waiting for transfers between devices: none -> 164 us  [the longest x24 153 us: partner(): return lax.ppermute(value, 'dp', [(i, i ^ 1 << bit) for i in range(dp)])]
    unnamed x80 -> x90, local copies, waits for them, and re-layouts: 125 us -> 32.9 us
    transpose x9 -> x2, local copies, waits for them, and re-layouts: 83.2 us -> 3.37 us  [collect_rows(): part.astype(bf16).reshape(dp, rows, ratio, cols).transpose(0, 2, 1, 3)]
    another operation x9, other arithmetic: 61.2 us -> 3.81 us  [the longest x6 3.51 us: gather_over_dp(): got = partner(jnp.stack([vals[k] for k in held]), bit, dp)]
    ppermute x0 -> x28, starting transfers between devices: none -> 43.9 us  [the longest x24 22.4 us: partner(): return lax.ppermute(value, 'dp', [(i, i ^ 1 << bit) for i in range(dp)])]
  transfers between devices with their start and end apart: 6 -> 32, of which waited for: 3 -> 17; matrix products, arithmetic and copies ran while one was open for 26% -> 37% of each run, Pallas kernels for 0% -> 0%
where the time goes in v1:
time: 499 us; the launch traced here: 490 us
  waiting for transfers between devices  227 us (45%)
  matrix products  116 us (23%)
  local copies, waits for them, and re-layouts  75.6 us (15%)
  starting transfers between devices  44.1 us (9%)
  between operations  14.8 us (3%)
  other arithmetic  12.5 us (3%)
    ppermute x24, waiting for transfers between devices, partner(): return lax.ppermute(value, 'dp', [(i, i ^ 1 << bit) for i in range(dp)])  153 us
    dot_general x9, matrix products, dot(): return lax.dot_general(a, b, dims, preferred_element_type=f32)  114 us
    unnamed x90, local copies, waits for them, and re-layouts  32.9 us
    all_gather x2, waiting for transfers between devices, spread_rows(): full = lax.all_gather(moved, 'mp', axis=0, tiled=False)  32.6 us
    reduce_scatter x2, waiting for transfers between devices, collect_rows(): lax.psum_scatter(part.reshape(mp * rows, cols), 'mp', scatter_dimension=0...  29.8 us
    ppermute x24, starting transfers between devices, partner(): return lax.ppermute(value, 'dp', [(i, i ^ 1 << bit) for i in range(dp)])  22.4 us
    ppermute x2, starting transfers between devices, spread_rows(): moved = lax.ppermute(block, ('dp', 'mp'), there)  12.6 us
    ppermute x2, waiting for transfers between devices, spread_rows(): moved = lax.ppermute(block, ('dp', 'mp'), there)  11.7 us
  transfers between devices with their start and end apart: 32, of which 17 were waited for; matrix products, arithmetic and copies ran while one was open for 37% of the time, Pallas kernels for 0%

profile of v1, /device:TPU:6, one launch (start us, length us, event | category | flops | bytes accessed | tf_op | source)
XLA Modules:
  0.0 489.5 jit_solution(17211362658382529422)
XLA Ops:
  7.2 5.4 %collective-permute-start = (bf16[256,512]{1,0:T(8,128)(2,1)}, bf16[256,512]{1,0:T(8,128)(2,1)S(1)}, u32[]{:S(2)}, u32[]{:S(2)}) collective-permute-start(bf16[256,512]{1,0:T(8,128)(2,1)} %param.8), channel_id=1, source_target_pairs={{0,0},{1,1},{2,10},{3,11},{4,20},{5,21},{6,30},{7,31},{8,2},{9,3},... | collective-permute-start | bytes 786440 | tf_op jit(solution)/shard_map/ppermute | solution.py:82
  12.6 6.7 %collective-permute-done = bf16[256,512]{1,0:T(8,128)(2,1)S(1)} collective-permute-done((bf16[256,512]{1,0:T(8,128)(2,1)}, bf16[256,512]{1,0:T(8,128)(2,1)S(1)}, u32[]{:S(2)}, u32[]{:S(2)}) %collective-permute-start) | collective-permute-done | bytes 262176 | tf_op jit(solution)/shard_map/ppermute | solution.py:82
  20.1 7.2 %collective-permute-start.14 = (bf16[256,512]{1,0:T(8,128)(2,1)}, bf16[256,512]{1,0:T(8,128)(2,1)S(1)}, u32[]{:S(2)}, u32[]{:S(2)}) collective-permute-start(bf16[256,512]{1,0:T(8,128)(2,1)} %param.9), channel_id=1, source_target_pairs={{0,0},{1,1},{2,10},{3,11},{4,20},{5,21},{6,30},{7,31},{8,2},{9,3},... | collective-permute-start | bytes 786440 | tf_op jit(solution)/shard_map/ppermute | solution.py:82
  27.3 5.0 %collective-permute-done.14 = bf16[256,512]{1,0:T(8,128)(2,1)S(1)} collective-permute-done((bf16[256,512]{1,0:T(8,128)(2,1)}, bf16[256,512]{1,0:T(8,128)(2,1)S(1)}, u32[]{:S(2)}, u32[]{:S(2)}) %collective-permute-start.14) | collective-permute-done | bytes 262176 | tf_op jit(solution)/shard_map/ppermute | solution.py:82
  35.3 6.4 %copy.22 = bf16[1024,2048]{0,1:T(8,128)(2,1)} copy(bf16[1024,2048]{1,0:T(8,128)(2,1)} %param.10) | data formatting | bytes 8388608 | tf_op args[2]
  41.8 6.4 %copy.25 = bf16[1024,2048]{0,1:T(8,128)(2,1)} copy(bf16[1024,2048]{1,0:T(8,128)(2,1)} %param.11) | data formatting | bytes 8388608 | tf_op args[3]
  61.0 29.4 %all-gather.7.cloned.1.call-done = bf16[2048,512]{1,0:T(8,128)(2,1)} async-done(((bf16[256,512]{1,0:T(8,128)(2,1)}), bf16[2048,512]{1,0:T(8,128)(2,1)}) %all-gather.7.cloned.1.call-update) | async-done | bytes 2097168 | tf_op jit(solution)/shard_map/all_gather | solution.py:83
  94.7 5.8 %broadcast_in_dim.7 = bf16[8,128,2048]{1,0,2:T(8,128)(2,1)S(1)} broadcast(bf16[8,2048]{0,1:T(8,128)(2,1)S(1)} %copy.24), dimensions={0,2} | broadcast | bytes 4227072 | tf_op jit(solution)/shard_map/broadcast_in_dim | solution.py:18
  100.5 5.0 %convolution_convert_fusion.1 = bf16[2048,1024]{0,1:T(8,128)(2,1)S(1)} fusion(bf16[1024,1024]{1,0:T(8,128)(2,1)S(1)} %bitcast.147, bf16[1024,2048]{0,1:T(8,128)(2,1)S(1)} %copy-done.6, bf16[256,8,8,128]{3,2,1,0:T(8,128)(2,1)S(1)} %bitcast.124), kind=kOutput, calls=%fused_computation.13 | convolution fusion | flops 4299161600 | bytes 14680064 | tf_op jit(solution)/shard_map/dot_general | solution.py:124
  106.4 5.8 %broadcast_in_dim.6 = bf16[8,128,2048]{1,0,2:T(8,128)(2,1)S(1)} broadcast(bf16[8,2048]{0,1:T(8,128)(2,1)S(1)} %copy.21), dimensions={0,2} | broadcast | bytes 4227072 | tf_op jit(solution)/shard_map/broadcast_in_dim | solution.py:18
  112.2 5.4 %convolution_convert_fusion.2 = bf16[2048,1024]{0,1:T(8,128)(2,1)S(1)} fusion(bf16[1024,1024]{1,0:T(8,128)(2,1)S(1)} %bitcast.148, bf16[1024,2048]{0,1:T(8,128)(2,1)S(1)} %copy-done.4, bf16[256,8,8,128]{3,2,1,0:T(8,128)(2,1)S(1)} %bitcast.127), kind=kOutput, calls=%fused_computation.14 | convolution fusion | flops 4299161600 | bytes 14680064 | tf_op jit(solution)/shard_map/dot_general | solution.py:124
  119.8 4.8 convolution_convert_fusion
  132.6 21.7 %collective-permute-done.1 = bf16[2,256,1024]{2,1,0:T(8,128)(2,1)S(1)} collective-permute-done((bf16[2,256,1024]{2,1,0:T(8,128)(2,1)S(1)}, bf16[2,256,1024]{2,1,0:T(8,128)(2,1)S(1)}, u32[]{:S(2)}, u32[]{:S(2)}) %collective-permute-start.1) | collective-permute-done | bytes 1048608 | tf_op jit(solution)/shard_map/ppermute | solution.py:22
  155.1 21.0 %collective-permute-done.15 = bf16[2,256,1024]{2,1,0:T(8,128)(2,1)S(1)} collective-permute-done((bf16[2,256,1024]{2,1,0:T(8,128)(2,1)S(1)}, bf16[2,256,1024]{2,1,0:T(8,128)(2,1)S(1)}, u32[]{:S(2)}, u32[]{:S(2)}) %collective-permute-start.15) | collective-permute-done | bytes 1048608 | tf_op jit(solution)/shard_map/ppermute | solution.py:22
  178.3 30.3 %collective-permute-done.6 = bf16[1,256,1024]{2,1,0:T(8,128)(2,1)S(1)} collective-permute-done((bf16[1,256,1024]{2,1,0:T(8,128)(2,1)S(1)}, bf16[1,256,1024]{2,1,0:T(8,128)(2,1)S(1)}, u32[]{:S(2)}, u32[]{:S(2)}) %collective-permute-start.6) | collective-permute-done | bytes 524320 | tf_op jit(solution)/shard_map/ppermute | solution.py:22
  209.8 10.1 %collective-permute-done.2 = bf16[1,256,1024]{2,1,0:T(8,128)(2,1)S(1)} collective-permute-done((bf16[1,256,1024]{2,1,0:T(8,128)(2,1)S(1)}, bf16[1,256,1024]{2,1,0:T(8,128)(2,1)S(1)}, u32[]{:S(2)}, u32[]{:S(2)}) %collective-permute-start.2) | collective-permute-done | bytes 524320 | tf_op jit(solution)/shard_map/ppermute | solution.py:22
  221.0 8.8 %collective-permute-done.16 = bf16[1,256,1024]{2,1,0:T(8,128)(2,1)S(1)} collective-permute-done((bf16[1,256,1024]{2,1,0:T(8,128)(2,1)S(1)}, bf16[1,256,1024]{2,1,0:T(8,128)(2,1)S(1)}, u32[]{:S(2)}, u32[]{:S(2)}) %collective-permute-start.16) | collective-permute-done | bytes 524320 | tf_op jit(solution)/shard_map/ppermute | solution.py:22
  232.0 11.0 %collective-permute-done.18 = bf16[1,256,1024]{2,1,0:T(8,128)(2,1)S(1)} collective-permute-done((bf16[1,256,1024]{2,1,0:T(8,128)(2,1)S(1)}, bf16[1,256,1024]{2,1,0:T(8,128)(2,1)S(1)}, u32[]{:S(2)}, u32[]{:S(2)}) %collective-permute-start.18) | collective-permute-done | bytes 524320 | tf_op jit(solution)/shard_map/ppermute | solution.py:22
  250.2 9.6 %collective-permute-done.11 = bf16[1,256,1024]{2,1,0:T(8,128)(2,1)S(1)} collective-permute-done((bf16[1,256,1024]{2,1,0:T(8,128)(2,1)S(1)}, bf16[1,256,1024]{2,1,0:T(8,128)(2,1)S(1)}, u32[]{:S(2)}, u32[]{:S(2)}) %collective-permute-start.11) | collective-permute-done | bytes 524320 | tf_op jit(solution)/shard_map/ppermute | solution.py:22
  263.9 7.1 %collective-permute-done.21 = bf16[1,256,1024]{2,1,0:T(8,128)(2,1)S(1)} collective-permute-done((bf16[1,256,1024]{2,1,0:T(8,128)(2,1)S(1)}, bf16[1,256,1024]{2,1,0:T(8,128)(2,1)S(1)}, u32[]{:S(2)}, u32[]{:S(2)}) %collective-permute-start.21) | collective-permute-done | bytes 524320 | tf_op jit(solution)/shard_map/ppermute | solution.py:22
  274.3 7.9 %collective-permute-done.25 = bf16[1,256,1024]{2,1,0:T(8,128)(2,1)S(1)} collective-permute-done((bf16[1,256,1024]{2,1,0:T(8,128)(2,1)S(1)}, bf16[1,256,1024]{2,1,0:T(8,128)(2,1)S(1)}, u32[]{:S(2)}, u32[]{:S(2)}) %collective-permute-start.25) | collective-permute-done | bytes 524320 | tf_op jit(solution)/shard_map/ppermute | solution.py:22
  283.9 21.4 %collective-permute-done.23 = bf16[1,256,1024]{2,1,0:T(8,128)(2,1)S(1)} collective-permute-done((bf16[1,256,1024]{2,1,0:T(8,128)(2,1)S(1)}, bf16[1,256,1024]{2,1,0:T(8,128)(2,1)S(1)}, u32[]{:S(2)}, u32[]{:S(2)}) %collective-permute-start.23) | collective-permute-done | bytes 524320 | tf_op jit(solution)/shard_map/ppermute | solution.py:22
  309.8 29.8 %convolution_convert_fusion.5 = bf16[1024,1024]{1,0:T(8,128)(2,1)} fusion(bf16[2048,1024]{1,0:T(8,128)(2,1)S(1)} %copy-done.8, bf16[256,1024]{1,0:T(8,128)(2,1)S(1)} %get-tuple-element.53, bf16[256,1024]{1,0:T(8,128)(2,1)S(1)} %get-tuple-element.52, bf16[256,1024]{1,0:T(8,128)(2,1)S(1)} %bitcast.153, bf16[256,1024]{1,0:T(8,128)(2,1)S(1)} %get-tuple-element.49, ...), kind=kOutput, calls=%fused_computation.27 | convolution fusion | flops 4329570304 | bytes 10485760 | tf_op jit(solution)/shard_map/dot_general | solution.py:124
  354.7 8.6 %fusion.6 = f32[1024,1024]{1,0:T(8,128)} fusion(bf16[1024,2048]{0,1:T(8,128)(2,1)S(1)} %copy-done.7, bf16[256,8,8,128]{3,2,1,0:T(8,128)(2,1)S(1)} %bitcast.126, bf16[256,1024]{1,0:T(8,128)(2,1)} %get-tuple-element.45, bf16[256,1024]{1,0:T(8,128)(2,1)S(1)} %get-tuple-element.44, bf16[256,1024]{1,0:T(8,128)(2,1)} %bitcast.157, ...), kind=kOutput, calls=%fused_computation.30 | convolution fusion | flops 4330618880 | bytes 16777216 | tf_op jit(solution)/shard_map/dot_general | solution.py:124
  363.3 13.4 %add_convert_fusion = bf16[1024,1024]{1,0:T(8,128)(2,1)} fusion(f32[1024,1024]{1,0:T(8,128)} %fusion.6, bf16[1024,2048]{0,1:T(8,128)(2,1)S(1)} %copy-done.5, bf16[256,8,8,128]{3,2,1,0:T(8,128)(2,1)S(1)} %bitcast.129, bf16[256,1024]{1,0:T(8,128)(2,1)} %get-tuple-element.37, bf16[256,1024]{1,0:T(8,128)(2,1)} %get-tuple-element.36, ...), kind=kOutput, calls=%fused_computation.11 | convolution fusion | flops 4332716032 | bytes 18874368 | tf_op jit(solution)/shard_map/dot_general | solution.py:124
  381.7 14.6 %fusion.1 = bf16[1024,2048]{0,1:T(8,128)(2,1)} fusion(bf16[1024,1024]{1,0:T(8,128)(2,1)} %bitcast.149, bf16[256,8,8,128]{3,2,1,0:T(8,128)(2,1)} %bitcast.128, bf16[256,1024]{1,0:T(8,128)(2,1)} %get-tuple-element.37, bf16[256,1024]{1,0:T(8,128)(2,1)} %get-tuple-element.36, bf16[256,1024]{1,0:T(8,128)(2,1)} %bitcast.162, bf16[256,1024]{1,0:T(8,128)(2,1)S(1)} %copy-done.22, ...), kind=kOutput, calls=%fused_computation.3 | convolution fusion | flops 4336910336 | bytes 14680064 | tf_op jit(solution)/shard_map/dot_general | solution.py:124
  400.3 29.8 %reduce-scatter.5.cloned.1.call-done = bf16[256,512]{1,0:T(8,128)(2,1)} async-done(((bf16[2048,512]{1,0:T(8,128)(2,1)}), bf16[256,512]{1,0:T(8,128)(2,1)}) %reduce-scatter.5.cloned.1.call-update) | async-done | bytes 262160 | tf_op jit(solution)/shard_map/reduce_scatter | solution.py:89
  430.2 5.0 %collective-permute-start.27 = (bf16[256,512]{1,0:T(8,128)(2,1)}, bf16[256,512]{1,0:T(8,128)(2,1)}, u32[]{:S(2)}, u32[]{:S(2)}) collective-permute-start(bf16[256,512]{1,0:T(8,128)(2,1)} %reduce-scatter.5.cloned.1.call-done), channel_id=1, source_target_pairs={{0,0},{1,1},{10,2},{11,3},{20,4},{21,5},{30,6},{31,7},{2,8},{3,9},... | collective-permute-start | bytes 786440 | tf_op jit(solution)/shard_map/ppermute | solution.py:92
  435.1 12.7 %fusion = bf16[1024,2048]{0,1:T(8,128)(2,1)} fusion(bf16[1024,1024]{1,0:T(8,128)(2,1)} %bitcast.150, bf16[256,8,8,128]{3,2,1,0:T(8,128)(2,1)} %bitcast.125, bf16[256,1024]{1,0:T(8,128)(2,1)} %get-tuple-element.45, bf16[256,1024]{1,0:T(8,128)(2,1)} %copy-done.35, bf16[256,1024]{1,0:T(8,128)(2,1)} %bitcast.158, bf16[256,1024]{1,0:T(8,128)(2,1)} %get-tuple-element.41, ...), kind=kOutput, calls=%fused_computation.1 | convolution fusion | flops 4336910336 | bytes 14680064 | tf_op jit(solution)/shard_map/dot_general | solution.py:124
  447.9 19.6 %multiply_convert_fusion = bf16[2048,1024]{1,0:T(8,128)(2,1)} fusion(bf16[1024,1024]{1,0:T(8,128)(2,1)S(1)} %bitcast.146, bf16[16,1024]{1,0:T(8,128)(2,1)S(1)} %copy-done.39, bf16[256,1024]{1,0:T(8,128)(2,1)S(1)} %copy-done.30, bf16[256,1024]{1,0:T(8,128)(2,1)S(1)} %copy-done.28, bf16[256,1024]{1,0:T(8,128)(2,1)S(1)} %bitcast.154, ...), kind=kOutput, calls=%fused_computation.4 | convolution fusion | flops 4336910336 | bytes 10518528 | tf_op jit(solution)/shard_map/dot_general | solution.py:124
  467.6 6.4 %copy.30 = bf16[1024,2048]{1,0:T(8,128)(2,1)} copy(bf16[1024,2048]{0,1:T(8,128)(2,1)} %fusion) | data formatting | bytes 8388608
  474.0 6.4 %copy.29 = bf16[1024,2048]{1,0:T(8,128)(2,1)} copy(bf16[1024,2048]{0,1:T(8,128)(2,1)} %fusion.1) | data formatting | bytes 8388608
  (187 shorter events, 86.3 us)
Async XLA Ops:
  7.2 49.5 %all-gather.5.cloned.1.call-start = ((), (), s32[]{:S(2)}) async-start(), calls=%async_computation.4 | async-start | bytes 2359296 | tf_op jit(solution)/shard_map/all_gather | solution.py:83
  7.2 12.1 %collective-permute-start = (bf16[256,512]{1,0:T(8,128)(2,1)}, bf16[256,512]{1,0:T(8,128)(2,1)S(1)}, u32[]{:S(2)}, u32[]{:S(2)}) collective-permute-start(bf16[256,512]{1,0:T(8,128)(2,1)} %param.8), channel_id=1, source_target_pairs={{0,0},{1,1},{2,10},{3,11},{4,20},{5,21},{6,30},{7,31},{8,2},{9,3},... | collective-permute-start | bytes 786440 | tf_op jit(solution)/shard_map/ppermute | solution.py:82
  20.1 70.3 %all-gather.7.cloned.1.call-start = ((), (), s32[]{:S(2)}) async-start(), calls=%async_computation.5 | async-start | bytes 2359296 | tf_op jit(solution)/shard_map/all_gather | solution.py:83
  20.1 12.2 %collective-permute-start.14 = (bf16[256,512]{1,0:T(8,128)(2,1)}, bf16[256,512]{1,0:T(8,128)(2,1)S(1)}, u32[]{:S(2)}, u32[]{:S(2)}) collective-permute-start(bf16[256,512]{1,0:T(8,128)(2,1)} %param.9), channel_id=1, source_target_pairs={{0,0},{1,1},{2,10},{3,11},{4,20},{5,21},{6,30},{7,31},{8,2},{9,3},... | collective-permute-start | bytes 786440 | tf_op jit(solution)/shard_map/ppermute | solution.py:82
  33.0 363.3 %reduce-scatter.3.cloned.1.call-start = ((), (), s32[]{:S(2)}) async-start(), calls=%async_computation.2 | async-start | bytes 2359296 | tf_op jit(solution)/shard_map/reduce_scatter | solution.py:89
  105.7 26.1 %collective-permute-start.5 = (bf16[2,256,1024]{2,1,0:T(8,128)(2,1)S(1)}, bf16[2,256,1024]{2,1,0:T(8,128)(2,1)S(1)}, u32[]{:S(2)}, u32[]{:S(2)}) collective-permute-start(bf16[2,256,1024]{2,1,0:T(8,128)(2,1)S(1)} %pad_maximum_fusion.4), channel_id=1, source_target_pairs={{0,8},{8,0},{16,24},{24,16},{1,9},{9,1},{17,25},{25,17},{2,10},{10... | collective-permute-start | bytes 3145736 | tf_op jit(solution)/shard_map/ppermute | solution.py:22
  117.8 36.5 %collective-permute-start.1 = (bf16[2,256,1024]{2,1,0:T(8,128)(2,1)S(1)}, bf16[2,256,1024]{2,1,0:T(8,128)(2,1)S(1)}, u32[]{:S(2)}, u32[]{:S(2)}) collective-permute-start(bf16[2,256,1024]{2,1,0:T(8,128)(2,1)S(1)} %pad_maximum_fusion.3), channel_id=1, source_target_pairs={{0,8},{8,0},{16,24},{24,16},{1,9},{9,1},{17,25},{25,17},{2,10},{10... | collective-permute-start | bytes 3145736 | tf_op jit(solution)/shard_map/ppermute | solution.py:22
  124.8 51.3 %collective-permute-start.15 = (bf16[2,256,1024]{2,1,0:T(8,128)(2,1)S(1)}, bf16[2,256,1024]{2,1,0:T(8,128)(2,1)S(1)}, u32[]{:S(2)}, u32[]{:S(2)}) collective-permute-start(bf16[2,256,1024]{2,1,0:T(8,128)(2,1)S(1)} %pad_maximum_fusion.7), channel_id=1, source_target_pairs={{0,8},{8,0},{16,24},{24,16},{1,9},{9,1},{17,25},{25,17},{2,10},{10... | collective-permute-start | bytes 3145736 | tf_op jit(solution)/shard_map/ppermute | solution.py:22
  126.4 50.4 %collective-permute-start.7 = (bf16[2,256,1024]{2,1,0:T(8,128)(2,1)S(1)}, bf16[2,256,1024]{2,1,0:T(8,128)(2,1)S(1)}, u32[]{:S(2)}, u32[]{:S(2)}) collective-permute-start(bf16[2,256,1024]{2,1,0:T(8,128)(2,1)S(1)} %stack.85), channel_id=1, source_target_pairs={{0,16},{8,24},{16,0},{24,8},{1,17},{9,25},{17,1},{25,9},{2,18},{10... | collective-permute-start | bytes 3145736 | tf_op jit(solution)/shard_map/ppermute | solution.py:22
  127.2 82.6 %collective-permute-start.3 = (bf16[2,256,1024]{2,1,0:T(8,128)(2,1)S(1)}, bf16[2,256,1024]{2,1,0:T(8,128)(2,1)S(1)}, u32[]{:S(2)}, u32[]{:S(2)}) collective-permute-start(bf16[2,256,1024]{2,1,0:T(8,128)(2,1)S(1)} %stack.84), channel_id=1, source_target_pairs={{0,16},{8,24},{16,0},{24,8},{1,17},{9,25},{17,1},{25,9},{2,18},{10... | collective-permute-start | bytes 3145736 | tf_op jit(solution)/shard_map/ppermute | solution.py:22
  131.8 89.2 %collective-permute-start.17 = (bf16[2,256,1024]{2,1,0:T(8,128)(2,1)S(1)}, bf16[2,256,1024]{2,1,0:T(8,128)(2,1)S(1)}, u32[]{:S(2)}, u32[]{:S(2)}) collective-permute-start(bf16[2,256,1024]{2,1,0:T(8,128)(2,1)S(1)} %stack.86), channel_id=1, source_target_pairs={{0,16},{8,24},{16,0},{24,8},{1,17},{9,25},{17,1},{25,9},{2,18},{10... | collective-permute-start | bytes 3145736 | tf_op jit(solution)/shard_map/ppermute | solution.py:22
  154.3 54.4 %collective-permute-start.6 = (bf16[1,256,1024]{2,1,0:T(8,128)(2,1)S(1)}, bf16[1,256,1024]{2,1,0:T(8,128)(2,1)S(1)}, u32[]{:S(2)}, u32[]{:S(2)}) collective-permute-start(bf16[1,256,1024]{2,1,0:T(8,128)(2,1)S(1)} %add_convert_fusion.4), channel_id=1, source_target_pairs={{0,16},{8,24},{16,0},{24,8},{1,17},{9,25},{17,1},{25,9},{2,18},{10... | collective-permute-start | bytes 1572872 | tf_op jit(solution)/shard_map/ppermute | solution.py:22
  176.0 43.9 %collective-permute-start.2 = (bf16[1,256,1024]{2,1,0:T(8,128)(2,1)S(1)}, bf16[1,256,1024]{2,1,0:T(8,128)(2,1)S(1)}, u32[]{:S(2)}, u32[]{:S(2)}) collective-permute-start(bf16[1,256,1024]{2,1,0:T(8,128)(2,1)S(1)} %add_convert_fusion.6), channel_id=1, source_target_pairs={{0,16},{8,24},{16,0},{24,8},{1,17},{9,25},{17,1},{25,9},{2,18},{10... | collective-permute-start | bytes 1572872 | tf_op jit(solution)/shard_map/ppermute | solution.py:22
  176.8 53.0 %collective-permute-start.16 = (bf16[1,256,1024]{2,1,0:T(8,128)(2,1)S(1)}, bf16[1,256,1024]{2,1,0:T(8,128)(2,1)S(1)}, u32[]{:S(2)}, u32[]{:S(2)}) collective-permute-start(bf16[1,256,1024]{2,1,0:T(8,128)(2,1)S(1)} %add_convert_fusion.2), channel_id=1, source_target_pairs={{0,16},{8,24},{16,0},{24,8},{1,17},{9,25},{17,1},{25,9},{2,18},{10... | collective-permute-start | bytes 1572872 | tf_op jit(solution)/shard_map/ppermute | solution.py:22
  209.1 21.8 %collective-permute-start.8 = (bf16[1,256,1024]{2,1,0:T(8,128)(2,1)S(1)}, bf16[1,256,1024]{2,1,0:T(8,128)(2,1)S(1)}, u32[]{:S(2)}, u32[]{:S(2)}) collective-permute-start(bf16[1,256,1024]{2,1,0:T(8,128)(2,1)S(1)} %get-tuple-element.27), channel_id=1, source_target_pairs={{0,8},{8,0},{16,24},{24,16},{1,9},{9,1},{17,25},{25,17},{2,10},{10... | collective-permute-start | bytes 1572872 | tf_op jit(solution)/shard_map/ppermute | solution.py:22
  220.4 11.4 %collective-permute-start.4 = (bf16[1,256,1024]{2,1,0:T(8,128)(2,1)S(1)}, bf16[1,256,1024]{2,1,0:T(8,128)(2,1)S(1)}, u32[]{:S(2)}, u32[]{:S(2)}) collective-permute-start(bf16[1,256,1024]{2,1,0:T(8,128)(2,1)S(1)} %get-tuple-element.23), channel_id=1, source_target_pairs={{0,8},{8,0},{16,24},{24,16},{1,9},{9,1},{17,25},{25,17},{2,10},{10... | collective-permute-start | bytes 1572872 | tf_op jit(solution)/shard_map/ppermute | solution.py:22
  230.3 12.7 %collective-permute-start.18 = (bf16[1,256,1024]{2,1,0:T(8,128)(2,1)S(1)}, bf16[1,256,1024]{2,1,0:T(8,128)(2,1)S(1)}, u32[]{:S(2)}, u32[]{:S(2)}) collective-permute-start(bf16[1,256,1024]{2,1,0:T(8,128)(2,1)S(1)} %get-tuple-element.19), channel_id=1, source_target_pairs={{0,8},{8,0},{16,24},{24,16},{1,9},{9,1},{17,25},{25,17},{2,10},{10... | collective-permute-start | bytes 1572872 | tf_op jit(solution)/shard_map/ppermute | solution.py:22
  244.9 14.9 %collective-permute-start.11 = (bf16[1,256,1024]{2,1,0:T(8,128)(2,1)S(1)}, bf16[1,256,1024]{2,1,0:T(8,128)(2,1)S(1)}, u32[]{:S(2)}, u32[]{:S(2)}) collective-permute-start(bf16[1,256,1024]{2,1,0:T(8,128)(2,1)S(1)} %get-tuple-element.48), channel_id=1, source_target_pairs={{0,8},{8,0},{16,24},{24,16},{1,9},{9,1},{17,25},{25,17},{2,10},{10... | collective-permute-start | bytes 1572872 | tf_op jit(solution)/shard_map/ppermute | solution.py:22
  245.5 16.7 %collective-permute-start.9 = (bf16[1,256,1024]{2,1,0:T(8,128)(2,1)S(1)}, bf16[1,256,1024]{2,1,0:T(8,128)(2,1)S(1)}, u32[]{:S(2)}, u32[]{:S(2)}) collective-permute-start(bf16[1,256,1024]{2,1,0:T(8,128)(2,1)S(1)} %get-tuple-element.47), channel_id=1, source_target_pairs={{0,16},{8,24},{16,0},{24,8},{1,17},{9,25},{17,1},{25,9},{2,18},{10... | collective-permute-start | bytes 1572872 | tf_op jit(solution)/shard_map/ppermute | solution.py:22
  247.3 24.4 %collective-permute-start.19 = (bf16[1,256,1024]{2,1,0:T(8,128)(2,1)S(1)}, bf16[1,256,1024]{2,1,0:T(8,128)(2,1)S(1)}, u32[]{:S(2)}, u32[]{:S(2)}) collective-permute-start(bf16[1,256,1024]{2,1,0:T(8,128)(2,1)S(1)} %get-tuple-element.31), channel_id=1, source_target_pairs={{0,16},{8,24},{16,0},{24,8},{1,17},{9,25},{17,1},{25,9},{2,18},{10... | collective-permute-start | bytes 1572872 | tf_op jit(solution)/shard_map/ppermute | solution.py:22
  248.7 22.3 %collective-permute-start.21 = (bf16[1,256,1024]{2,1,0:T(8,128)(2,1)S(1)}, bf16[1,256,1024]{2,1,0:T(8,128)(2,1)S(1)}, u32[]{:S(2)}, u32[]{:S(2)}) collective-permute-start(bf16[1,256,1024]{2,1,0:T(8,128)(2,1)S(1)} %get-tuple-element.32), channel_id=1, source_target_pairs={{0,8},{8,0},{16,24},{24,16},{1,9},{9,1},{17,25},{25,17},{2,10},{10... | collective-permute-start | bytes 1572872 | tf_op jit(solution)/shard_map/ppermute | solution.py:22
  259.9 47.0 %collective-permute-start.12 = (bf16[2,256,1024]{2,1,0:T(8,128)(2,1)S(1)}, bf16[2,256,1024]{2,1,0:T(8,128)(2,1)S(1)}, u32[]{:S(2)}, u32[]{:S(2)}) collective-permute-start(bf16[2,256,1024]{2,1,0:T(8,128)(2,1)S(1)} %pad_maximum_fusion.6), channel_id=1, source_target_pairs={{0,16},{8,24},{16,0},{24,8},{1,17},{9,25},{17,1},{25,9},{2,18},{10... | collective-permute-start | bytes 3145736 | tf_op jit(solution)/shard_map/ppermute | solution.py:22
  261.7 20.6 %collective-permute-start.25 = (bf16[1,256,1024]{2,1,0:T(8,128)(2,1)S(1)}, bf16[1,256,1024]{2,1,0:T(8,128)(2,1)S(1)}, u32[]{:S(2)}, u32[]{:S(2)}) collective-permute-start(bf16[1,256,1024]{2,1,0:T(8,128)(2,1)S(1)} %get-tuple-element.40), channel_id=1, source_target_pairs={{0,8},{8,0},{16,24},{24,16},{1,9},{9,1},{17,25},{25,17},{2,10},{10... | collective-permute-start | bytes 1572872 | tf_op jit(solution)/shard_map/ppermute | solution.py:22
  262.4 46.1 %collective-permute-start.10 = (bf16[2,256,1024]{2,1,0:T(8,128)(2,1)S(1)}, bf16[2,256,1024]{2,1,0:T(8,128)(2,1)S(1)}, u32[]{:S(2)}, u32[]{:S(2)}) collective-permute-start(bf16[2,256,1024]{2,1,0:T(8,128)(2,1)S(1)} %pad_maximum_fusion.5), channel_id=1, source_target_pairs={{0,8},{8,0},{16,24},{24,16},{1,9},{9,1},{17,25},{25,17},{2,10},{10... | collective-permute-start | bytes 3145736 | tf_op jit(solution)/shard_map/ppermute | solution.py:22
  271.0 34.3 %collective-permute-start.23 = (bf16[1,256,1024]{2,1,0:T(8,128)(2,1)S(1)}, bf16[1,256,1024]{2,1,0:T(8,128)(2,1)S(1)}, u32[]{:S(2)}, u32[]{:S(2)}) collective-permute-start(bf16[1,256,1024]{2,1,0:T(8,128)(2,1)S(1)} %get-tuple-element.39), channel_id=1, source_target_pairs={{0,16},{8,24},{16,0},{24,8},{1,17},{9,25},{17,1},{25,9},{2,18},{10... | collective-permute-start | bytes 1572872 | tf_op jit(solution)/shard_map/ppermute | solution.py:22
  271.7 73.0 %collective-permute-start.22 = (bf16[2,256,1024]{2,1,0:T(8,128)(2,1)S(1)}, bf16[2,256,1024]{2,1,0:T(8,128)(2,1)}, u32[]{:S(2)}, u32[]{:S(2)}) collective-permute-start(bf16[2,256,1024]{2,1,0:T(8,128)(2,1)S(1)} %pad_maximum_fusion.9), channel_id=1, source_target_pairs={{0,16},{8,24},{16,0},{24,8},{1,17},{9,25},{17,1},{25,9},{2,18},{10... | collective-permute-start | bytes 3145736 | tf_op jit(solution)/shard_map/ppermute | solution.py:22
  282.3 64.9 %collective-permute-start.20 = (bf16[2,256,1024]{2,1,0:T(8,128)(2,1)}, bf16[2,256,1024]{2,1,0:T(8,128)(2,1)}, u32[]{:S(2)}, u32[]{:S(2)}) collective-permute-start(bf16[2,256,1024]{2,1,0:T(8,128)(2,1)} %pad_maximum_fusion.8), channel_id=1, source_target_pairs={{0,8},{8,0},{16,24},{24,16},{1,9},{9,1},{17,25},{25,17},{2,10},{10... | collective-permute-start | bytes 3145736 | tf_op jit(solution)/shard_map/ppermute | solution.py:22
  305.3 44.8 %collective-permute-start.26 = (bf16[2,256,1024]{2,1,0:T(8,128)(2,1)}, bf16[2,256,1024]{2,1,0:T(8,128)(2,1)}, u32[]{:S(2)}, u32[]{:S(2)}) collective-permute-start(bf16[2,256,1024]{2,1,0:T(8,128)(2,1)} %pad_maximum_fusion.11), channel_id=1, source_target_pairs={{0,16},{8,24},{16,0},{24,8},{1,17},{9,25},{17,1},{25,9},{2,18},{10... | collective-permute-start | bytes 3145736 | tf_op jit(solution)/shard_map/ppermute | solution.py:22
  306.9 45.3 %collective-permute-start.24 = (bf16[2,256,1024]{2,1,0:T(8,128)(2,1)}, bf16[2,256,1024]{2,1,0:T(8,128)(2,1)}, u32[]{:S(2)}, u32[]{:S(2)}) collective-permute-start(bf16[2,256,1024]{2,1,0:T(8,128)(2,1)} %pad_maximum_fusion.10), channel_id=1, source_target_pairs={{0,8},{8,0},{16,24},{24,16},{1,9},{9,1},{17,25},{25,17},{2,10},{10... | collective-permute-start | bytes 3145736 | tf_op jit(solution)/shard_map/ppermute | solution.py:22
  344.6 85.5 %reduce-scatter.5.cloned.1.call-start = ((), (), s32[]{:S(2)}) async-start(), calls=%async_computation.3 | async-start | bytes 2359296 | tf_op jit(solution)/shard_map/reduce_scatter | solution.py:89
  396.4 84.1 %collective-permute-start.13 = (bf16[256,512]{1,0:T(8,128)(2,1)}, bf16[256,512]{1,0:T(8,128)(2,1)S(1)}, u32[]{:S(2)}, u32[]{:S(2)}) collective-permute-start(bf16[256,512]{1,0:T(8,128)(2,1)} %reduce-scatter.3.cloned.1.call-done), channel_id=1, source_target_pairs={{0,0},{1,1},{10,2},{11,3},{20,4},{21,5},{30,6},{31,7},{2,8},{3,9},... | collective-permute-start | bytes 786440 | tf_op jit(solution)/shard_map/ppermute | solution.py:92
  430.2 50.3 %collective-permute-start.27 = (bf16[256,512]{1,0:T(8,128)(2,1)}, bf16[256,512]{1,0:T(8,128)(2,1)}, u32[]{:S(2)}, u32[]{:S(2)}) collective-permute-start(bf16[256,512]{1,0:T(8,128)(2,1)} %reduce-scatter.5.cloned.1.call-done), channel_id=1, source_target_pairs={{0,0},{1,1},{10,2},{11,3},{20,4},{21,5},{30,6},{31,7},{2,8},{3,9},... | collective-permute-start | bytes 786440 | tf_op jit(solution)/shard_map/ppermute | solution.py:92
  (41 other events, 827.4 us)
Sparse Core Ops, SparseCore 0:
  20.2 36.4 all-gather.4
  58.9 31.4 all-gather.6
  344.7 35.4 reduce-scatter.2
  382.9 47.1 reduce-scatter.4
